TPU v7x, 256 devices: a whole 4x4x8 slice. The times are simulated.
256 devices in a mesh: cells: 64 (over y, z_lo, x), bands: 4 (over z_hi, core).
Axes of the slice: x: 4, y: 4, z: 8 (z_hi: 2, z_lo: 4; z = z_hi * 4 + z_lo), core: 2. Of those that a mesh axis runs over, the one named last changes fastest.
Arguments:
- waves: bfloat16 [256, 131072], P('bands', 'cells'), may hold values from -6 to 6
- stiffness: float32 [125, 125], replicated, as said below
- cell_scale: float32 [8192], P('cells'), may hold values from 0.5 to 4
- potential: float32 [131072], P('cells'), may hold values from -2 to 2
- connect: int32 [125, 8192], P(None, 'cells'), may hold values from 0 to 3071
- live_cells: int32 [64], P('cells'), may hold values from 16 to 128, as said below
- shared: int32 [64, 2, 512], P('cells'), may hold values from 0 to 2047
- window: float32 [2], replicated, may hold values from 1 to 4
Outputs:
- filtered: float32 [256, 131072], P('bands', 'cells')
- projected: float32 [256, 256], P('cells', 'bands')
Inputs may be any that keep to these rules, and one draw needn't show every extreme that they name: `live_cells`: at least one partition has all 128 slots live. `stiffness`: symmetric positive definite.
All inputs are finite; a program needn't handle non-finite values.
Results may differ from a plain program's by a relative error of at most 0.0037.
Values may be sent and summed in bfloat16 or wider, within the bound.
No kernel may reach another device: no remote copies, remote signals or barrier semaphores. Data moves between devices by JAX's collectives and lax.ppermute only.
A program may use at most 64 MiB of HBM per device.

v0:
```python
import math

import jax
import jax.numpy as jnp
from jax import lax
from jax.sharding import PartitionSpec as P

sigma_one = -0.5
sigma_two = 1.0 / (2.0 / sigma_one - sigma_one)


def with_halo(block, sides, width):
    for axis, dim in sides:
        count = lax.axis_size(axis)
        forward = [(i, i + 1) for i in range(count - 1)]
        backward = [(target, source) for source, target in forward]
        low = lax.ppermute(
            lax.slice_in_dim(block, block.shape[dim] - width, None, axis=dim), axis, forward
        )
        high = lax.ppermute(lax.slice_in_dim(block, 0, width, axis=dim), axis, backward)
        block = jnp.concatenate([low, block, high], axis=dim)
    return block


def local(waves, stiffness, cell_scale, potential, connect, live_cells, shared, window):
    columns, node_dev = waves.shape
    ghost = shared.shape[2]
    capacity = connect.shape[1]
    shared_rows = shared[0]
    live_count = live_cells[0]
    stiff_rounded = stiffness.astype(jnp.bfloat16)
    center = window[0]
    half_width = window[1]
    block_size = math.gcd(capacity, 128)
    block_turns = capacity // block_size
    potential_row = potential[None, :]

    def with_ghosts(owned):
        packed = jnp.concatenate([owned[:, shared_rows[0]], owned[:, shared_rows[1]]], axis=1)
        bordered = with_halo(packed, (("cells", 1),), ghost)
        return jnp.concatenate([bordered[:, :ghost], owned, bordered[:, 3 * ghost :]], axis=1)

    def assemble(totals):
        packed = jnp.concatenate([totals[:, :ghost], totals[:, ghost + node_dev :]], axis=1)
        bordered = with_halo(packed, (("cells", 1),), ghost)
        owned = totals[:, ghost : ghost + node_dev]
        return (
            owned.at[:, shared_rows[0]]
            .add(bordered[:, :ghost])
            .at[:, shared_rows[1]]
            .add(bordered[:, 3 * ghost :])
        )

    def cell_terms(extended):

        def one_block(turn, totals):
            first_cell = turn * block_size
            alive = (first_cell + jnp.arange(block_size) < live_count).astype(jnp.float32)
            weight = cell_scale * alive
            gathered = extended[:, connect]
            product = jnp.einsum(
                "ij,wjb->wib", stiff_rounded, gathered, preferred_element_type=jnp.float32
            )
            return totals.at[:, connect.reshape(-1)].add(
                (product * weight[None, None, :]).reshape(columns, -1)
            )

        empty = jnp.zeros((columns, extended.shape[1]), jnp.float32)
        return lax.fori_loop(0, block_turns, one_block, empty)

    waves32 = waves.astype(jnp.float32)
    applied_x = assemble(cell_terms(with_ghosts(waves))) + potential_row * waves32
    first_pass = ((applied_x - center * waves32) * (sigma_one / half_width)).astype(jnp.bfloat16)
    first32 = first_pass.astype(jnp.float32)
    applied_y = assemble(cell_terms(with_ghosts(first_pass))) + potential_row * first32
    filtered = (applied_y - center * first32) * (
        2.0 * sigma_two / half_width
    ) - sigma_one * sigma_two * waves32
    wave_rounded = filtered.astype(jnp.bfloat16)
    applied = assemble(cell_terms(with_ghosts(wave_rounded))) + potential_row * filtered
    apply_rounded = applied.astype(jnp.bfloat16)
    cell_count = lax.axis_size("cells")
    band_count = lax.axis_size("bands")
    inverse_total = 1.0 / (node_dev * cell_count)
    waves_all = columns * band_count
    own_rows = waves_all // cell_count
    swapped = (
        lax.all_to_all(wave_rounded, "bands", split_axis=1, concat_axis=0, tiled=True),
        lax.all_to_all(apply_rounded, "bands", split_axis=1, concat_axis=0, tiled=True),
    )
    left_side, right_side = swapped
    partial_value = (
        jnp.einsum("wn,vn->wv", left_side, right_side, preferred_element_type=jnp.float32)
        * inverse_total
    )
    arranged = partial_value.reshape(cell_count, own_rows, band_count, columns).transpose(
        0, 2, 1, 3
    )
    arranged = arranged.reshape(cell_count * band_count * own_rows, columns)
    projected = lax.psum_scatter(arranged, ("cells", "bands"), scatter_dimension=0, tiled=True)
    return (filtered, projected)


def solution(mesh):
    return jax.shard_map(
        local,
        mesh=mesh,
        in_specs=(
            P("bands", "cells"),
            P(),
            P("cells"),
            P("cells"),
            P(None, "cells"),
            P("cells"),
            P("cells", None, None),
            P(),
        ),
        out_specs=(P("bands", "cells"), P("cells", "bands")),
        check_vma=False,
    )
```

profile of v0, /device:TPU:2, one launch (start us, length us, event | category | flops | bytes accessed | tf_op | source)
XLA Modules:
  0.0 876.6 jit_solution(12638549431420464733)
XLA Ops:
  22.9 33.0 %gather_fusion.2 = bf16[16000,64]{1,0:T(8,128)(2,1)} fusion(bf16[64,3072]{0,1:T(8,128)(2,1)S(1)} %pad_maximum_fusion, s32[16384]{0:T(1024)S(1)} %pad_clamp_fusion), kind=kCustom, calls=%fused_computation.2 | custom fusion | bytes 4160000 | tf_op jit(solution)/shard_map/while/body/eval_jaxpr/gather | solution.py:60
  55.9 7.4 copy.39
  66.0 5.7 copy.40
  71.6 6.5 copy.63
  78.1 6.8 copy.41
  84.9 88.3 %scatter_custom_fusion = f32[64,3072]{0,1:T(8,128)S(1)} fusion(s32[16000]{0:T(1024)S(1)} %fusion.30, f32[16000,64]{1,0:T(8,128)} %copy.41, f32[]{:T(128)} %constant.22.clone.1), kind=kCustom, calls=%fused_computation.49 | custom fusion | flops 1024000 | bytes 786944 | tf_op jit(solution)/shard_map/while/body/eval_jaxpr/scatter-add | solution.py:64
  182.6 4.3 scatter_custom_fusion.1
  187.7 3.8 scatter_custom_fusion.2
  202.0 4.7 collective-permute-done.5
  206.8 33.0 %gather_fusion.5 = bf16[16000,64]{1,0:T(8,128)(2,1)} fusion(bf16[64,3072]{0,1:T(8,128)(2,1)S(1)} %pad_maximum_fusion.1, s32[16384]{0:T(1024)S(1)} %pad_clamp_fusion), kind=kCustom, calls=%fused_computation.5 | custom fusion | bytes 4160000 | tf_op jit(solution)/shard_map/while/body/eval_jaxpr/gather | solution.py:60
  239.8 7.3 copy.43
  249.8 5.7 copy.44
  255.5 6.5 copy.62
  261.9 6.8 copy.45
  268.7 88.3 %scatter_custom_fusion.3 = f32[64,3072]{0,1:T(8,128)S(1)} fusion(s32[16000]{0:T(1024)} %copy-done.3, f32[16000,64]{1,0:T(8,128)} %copy.45, f32[]{:T(128)} %constant.22.clone.1), kind=kCustom, calls=%fused_computation.47 | custom fusion | flops 1024000 | bytes 786944 | tf_op jit(solution)/shard_map/while/body/eval_jaxpr/scatter-add | solution.py:64
  357.1 4.5 collective-permute-start.6
  365.4 5.5 scatter_custom_fusion.4
  371.9 5.3 scatter_custom_fusion.5
  382.1 5.1 collective-permute-start.8
  390.0 7.6 all-to-all-start
  397.8 33.0 %gather_fusion.8 = bf16[16000,64]{1,0:T(8,128)(2,1)} fusion(bf16[64,3072]{0,1:T(8,128)(2,1)S(1)} %pad_maximum_fusion.2, s32[16384]{0:T(1024)S(1)} %pad_clamp_fusion), kind=kCustom, calls=%fused_computation.8 | custom fusion | bytes 4160000 | tf_op jit(solution)/shard_map/while/body/eval_jaxpr/gather | solution.py:60
  430.7 7.9 copy.47
  438.7 4.2 multiply_bitcast_fusion
  442.9 5.7 copy.48
  448.6 6.4 copy.61
  455.0 6.8 copy.49
  461.8 89.2 %scatter_custom_fusion.6 = f32[64,3072]{0,1:T(8,128)} fusion(s32[16000]{0:T(1024)} %copy-done.3, f32[16000,64]{1,0:T(8,128)} %copy.49, f32[]{:T(128)} %constant.22.clone.1), kind=kCustom, calls=%fused_computation.45 | custom fusion | flops 1024000 | bytes 786944 | tf_op jit(solution)/shard_map/while/body/eval_jaxpr/scatter-add | solution.py:64
  552.1 4.4 collective-permute-start.10
  562.7 3.8 scatter_custom_fusion.7
  567.2 3.8 scatter_custom_fusion.8
  571.3 19.3 %all_to_all.38 = bf16[64,4,512]{2,0,1:T(8,128)(2,1)S(1)} all-to-all(bf16[64,4,512]{2,0,1:T(8,128)(2,1)S(1)} %copy.50), channel_id=1, replica_groups=mesh['cells'=64,'bands'=4] {'bands'}, dimensions={1} | all-to-all | bytes 524288 | tf_op jit(solution)/shard_map/all_to_all | solution.py:89
  593.2 274.9 %all-reduce.3.cloned.1.call-done = f32[1024,64]{1,0:T(8,128)} async-done(((f32[1024,64]{1,0:T(8,128)}), f32[1024,64]{1,0:T(8,128)}) %all-reduce.3.cloned.1.call-update) | async-done | bytes 262160
  (81 shorter events, 64.6 us)
Async XLA Ops:
  7.2 12.7 %copy-start.1 = (s32[125,128]{1,0:T(8,128)S(1)}, s32[125,128]{1,0:T(8,128)}, u32[]{:S(2)}) copy-start(s32[125,128]{1,0:T(8,128)} %param.12) | copy-start | bytes 192004
  7.2 12.9 %copy-start.10 = (f32[128]{0:T(128)S(1)}, f32[128]{0:T(128)}, u32[]{:S(2)}) copy-start(f32[128]{0:T(128)} %param.10) | copy-start | bytes 1540
  7.2 13.0 %copy-start.9 = (f32[2]{0:T(128)S(1)}, f32[2]{0:T(128)}, u32[]{:S(2)}) copy-start(f32[2]{0:T(128)} %param.15) | copy-start | bytes 28
  8.0 0.6 copy-start.4
  8.0 7.9 copy-start.5
  11.1 10.2 %collective-permute-start = (bf16[64,512]{0,1:T(8,128)(2,1)S(1)}, bf16[64,512]{0,1:T(8,128)(2,1)S(1)}, u32[]{:S(2)}, u32[]{:S(2)}) collective-permute-start(bf16[64,512]{0,1:T(8,128)(2,1)S(1)} %bitcast.116), channel_id=1, source_target_pairs={{0,4},{4,8},{8,12},{12,16},{16,20},{20,24},{24,28},{28,32},{32,36}... | collective-permute-start | bytes 196616 | tf_op jit(solution)/shard_map/ppermute | solution.py:17
  15.9 6.9 collective-permute-start.1
  20.1 64.8 %copy-start.3 = (s32[16000]{0:T(1024)}, s32[16000]{0:T(1024)S(1)}, u32[]{:S(2)}) copy-start(s32[16000]{0:T(1024)S(1)} %fusion.30) | copy-start | bytes 192004
  20.1 43.1 %copy-start.6 = (f32[128]{0:T(128)}, f32[128]{0:T(128)S(1)}, u32[]{:S(2)}) copy-start(f32[128]{0:T(128)S(1)} %compare_select_fusion.4) | copy-start | bytes 1540
  55.9 7.4 copy-start
  84.9 95.6 %copy-start.2 = (f32[2048]{0:T(1024)S(1)}, f32[2048]{0:T(1024)}, u32[]{:S(2)}) copy-start(f32[2048]{0:T(1024)} %param.11) | copy-start | bytes 24580
  174.0 8.6 collective-permute-start.2
  177.2 10.6 %collective-permute-start.3 = (f32[64,512]{0,1:T(8,128)}, f32[64,512]{0,1:T(8,128)S(1)}, u32[]{:S(2)}, u32[]{:S(2)}) collective-permute-start(f32[64,512]{0,1:T(8,128)} %get-tuple-element.70), channel_id=1, source_target_pairs={{4,0},{8,4},{12,8},{16,12},{20,16},{24,20},{28,24},{32,28},{36,32}... | collective-permute-start | bytes 393224 | tf_op jit(solution)/shard_map/ppermute | solution.py:20
  195.1 6.9 collective-permute-start.4
  198.8 7.9 collective-permute-start.5
  239.8 7.3 copy-start.7
  357.1 8.3 collective-permute-start.6
  361.6 10.4 %collective-permute-start.7 = (f32[64,512]{0,1:T(8,128)S(1)}, f32[64,512]{0,1:T(8,128)S(1)}, u32[]{:S(2)}, u32[]{:S(2)}) collective-permute-start(f32[64,512]{0,1:T(8,128)S(1)} %get-tuple-element.68), channel_id=1, source_target_pairs={{4,0},{8,4},{12,8},{16,12},{20,16},{24,20},{28,24},{32,28},{36,32}... | collective-permute-start | bytes 393224 | tf_op jit(solution)/shard_map/ppermute | solution.py:20
  382.1 15.5 %collective-permute-start.8 = (bf16[64,512]{0,1:T(8,128)(2,1)S(1)}, bf16[64,512]{0,1:T(8,128)(2,1)S(1)}, u32[]{:S(2)}, u32[]{:S(2)}) collective-permute-start(bf16[64,512]{0,1:T(8,128)(2,1)S(1)} %bitcast.119), channel_id=1, source_target_pairs={{0,4},{4,8},{8,12},{12,16},{16,20},{20,24},{24,28},{28,32},{32,36}... | collective-permute-start | bytes 196616 | tf_op jit(solution)/shard_map/ppermute | solution.py:17
  387.2 10.4 %collective-permute-start.9 = (bf16[64,512]{0,1:T(8,128)(2,1)S(1)}, bf16[64,512]{0,1:T(8,128)(2,1)S(1)}, u32[]{:S(2)}, u32[]{:S(2)}) collective-permute-start(bf16[64,512]{0,1:T(8,128)(2,1)S(1)} %bitcast.117), channel_id=1, source_target_pairs={{4,0},{8,4},{12,8},{16,12},{20,16},{24,20},{28,24},{32,28},{36,32}... | collective-permute-start | bytes 196616 | tf_op jit(solution)/shard_map/ppermute | solution.py:20
  390.0 181.3 %all-to-all-start = ((bf16[64,4,512]{2,0,1:T(8,128)(2,1)}), bf16[64,4,512]{2,0,1:T(8,128)(2,1)S(1)}, u32[]{:S(2)}, u32[]{:S(2)}) async-start(bf16[64,4,512]{2,0,1:T(8,128)(2,1)} %copy.46), calls=%async_computation | async-start | bytes 524288 | tf_op jit(solution)/shard_map/all_to_all | solution.py:88
  397.6 470.5 %all-reduce.3.cloned.1.call-start = ((), (), s32[]{:S(2)}) async-start(), calls=%async_computation.2 | async-start | bytes 1048576
  430.7 7.9 copy-start.8
  552.1 10.6 %collective-permute-start.10 = (f32[64,512]{0,1:T(8,128)S(1)}, f32[64,512]{0,1:T(8,128)S(1)}, u32[]{:S(2)}, u32[]{:S(2)}) collective-permute-start(f32[64,512]{0,1:T(8,128)S(1)} %get-tuple-element.67), channel_id=1, source_target_pairs={{0,4},{4,8},{8,12},{12,16},{16,20},{20,24},{24,28},{28,32},{32,36}... | collective-permute-start | bytes 393224 | tf_op jit(solution)/shard_map/ppermute | solution.py:17
  556.5 10.7 %collective-permute-start.11 = (f32[64,512]{0,1:T(8,128)S(1)}, f32[64,512]{0,1:T(8,128)S(1)}, u32[]{:S(2)}, u32[]{:S(2)}) collective-permute-start(f32[64,512]{0,1:T(8,128)S(1)} %get-tuple-element.66), channel_id=1, source_target_pairs={{4,0},{8,4},{12,8},{16,12},{20,16},{24,20},{28,24},{32,28},{36,32}... | collective-permute-start | bytes 393224 | tf_op jit(solution)/shard_map/ppermute | solution.py:20
Sparse Core Ops, SparseCore 0:
  592.2 275.8 all-reduce.2
where the time goes:
time: 886 us; the launch traced here: 877 us
  other arithmetic  301 us (34%)
  waiting for transfers between devices  289 us (33%)
  local copies, waits for them, and re-layouts  195 us (22%)
  starting transfers between devices  45.7 us (5%)
  blocking collectives  19.3 us (2%)
  between operations  16.8 us (2%)
  matrix products  9.85 us (1%)
    unnamed x2, waiting for transfers between devices  275 us
    scatter-add x3, other arithmetic, one_block(): totals.at[:, connect.reshape(-1)]  266 us
    gather x6, local copies, waits for them, and re-layouts, one_block(): gathered = extended[:, connect]  121 us
    scatter-add x6, other arithmetic, assemble(): return owned.at[:, shared_rows[0]].add(bordered[:, :ghost]).at[:, shared_...  26.6 us
    ppermute x6, starting transfers between devices, with_halo(): lax.ppermute(lax.slice_in_dim(block, block.shape[dim] - width, None, axis...  24.2 us
    unnamed x28, local copies, waits for them, and re-layouts  23.6 us
    reshape x3, local copies, waits for them, and re-layouts, one_block(): (product * weight[None, None, :]).reshape(columns, -1)  20.4 us
    all_to_all x1, blocking collectives, local(): lax.all_to_all(apply_rounded, 'bands', split_axis=1, concat_axis=0, tiled...  19.3 us
  transfers between devices with their start and end apart: 14, of which 10 were waited for; matrix products, arithmetic and copies ran while one was open for 21% of the time, Pallas kernels for 0%

commit v1 on v0

v1 whole, which is shorter than its diff:
```python
import jax
import jax.numpy as jnp
from jax import lax
from jax.experimental import pallas as pl
from jax.experimental.pallas import tpu as pltpu
from jax.sharding import PartitionSpec as P

sigma_one = -0.5
sigma_two = 1.0 / (2.0 / sigma_one - sigma_one)

LANES = 128
HALF = 64
GROUP = 8
PAIRS = GROUP // 2
STEP = 25

VMEM = pl.BlockSpec(memory_space=pltpu.VMEM)
SMEM = pl.BlockSpec(memory_space=pltpu.SMEM)
PARAMS = pltpu.CompilerParams(vmem_limit_bytes=56 << 20)
f32 = jnp.float32
bf16 = jnp.bfloat16


def shape_of(rows, lanes, dtype):
    return jax.ShapeDtypeStruct((rows, lanes), dtype)


def left_lanes():
    return lax.broadcasted_iota(jnp.int32, (1, LANES), 1) < HALF


def swap(x):
    return pltpu.roll(x, HALF, 1)


def pack(rows):
    half = rows.shape[0] // 2
    return jnp.where(left_lanes(), rows[:half], rows[half:])


def unpack(x):
    left = left_lanes()
    other = swap(x)
    return jnp.where(left, x, other), jnp.where(left, other, x)


def pick_rows(values, shared_ref, base, count, stage):
    left = left_lanes()

    def some(turn, carry):
        for step in range(8):
            k = turn * 8 + step
            one = values[pl.ds(shared_ref[base + k], 1), :]
            two = values[pl.ds(shared_ref[base + count + k], 1), :]
            stage[pl.ds(k, 1), :] = jnp.where(left, one, two)
        return carry

    lax.fori_loop(0, count // 8, some, 0)


def send_lists(values, shared_ref, low_ref, high_ref, stage):
    count = stage.shape[0]
    pick_rows(values, shared_ref, 0, count, stage)
    low_ref[...] = stage[...].astype(bf16)
    pick_rows(values, shared_ref, 2 * count, count, stage)
    high_ref[...] = stage[...].astype(bf16)


def prepare_kernel(shared_ref, waves_ref, rows_ref, low_ref, high_ref, stage):
    block = waves_ref[...].astype(f32)
    rows_ref[...] = jnp.transpose(jnp.concatenate([block, block], axis=0))
    send_lists(rows_ref, shared_ref, low_ref, high_ref, stage)


def cell_sums(live_ref, index_ref, scale_ref, stiff_ref, own_ref, low_ref, high_ref, x, g, p, acc):
    left = left_lanes()
    ghost = 2 * low_ref.shape[0]
    half = ghost // 2
    owned = own_ref.shape[0]
    nodes = 125
    capacity = scale_ref.shape[0]
    x[pl.ds(ghost, owned), :] = own_ref[...]
    for first, ref in ((0, low_ref), (ghost + owned, high_ref)):
        one, two = unpack(ref[...].astype(f32))
        x[pl.ds(first, half), :] = one
        x[pl.ds(first + half, half), :] = two
    for a in acc:
        a[...] = jnp.zeros_like(a)
    for q in range(PAIRS):
        g[q, 120:128, :] = jnp.zeros((8, LANES), f32)
    live = live_ref[0]

    def gather(i, base):
        for q in range(PAIRS):
            one = x[pl.ds(index_ref[base + i * capacity + 2 * q], 1), :]
            two = x[pl.ds(index_ref[base + i * capacity + 2 * q + 1], 1), :]
            g[q, pl.ds(i, 1), :] = jnp.where(left, one, two)

    def scatter(i, base):
        rows = [p[q, pl.ds(i, 1), :] for q in range(PAIRS)]
        for k in range(GROUP):
            acc[k][pl.ds(index_ref[base + i * capacity + k], 1), :] += rows[k // 2]

    def each_row(f):
        def some(turn, carry):
            for step in range(STEP):
                f(turn * STEP + step)
            return carry

        lax.fori_loop(0, nodes // STEP, some, 0)

    each_row(lambda i: gather(i, 0))
    stiff = stiff_ref[...]

    def one_group(turn, carry):
        base = turn * GROUP
        following = jnp.minimum(turn + 1, capacity // GROUP - 1) * GROUP
        for q in range(0, PAIRS, 2):
            both = jnp.concatenate([g[q].astype(bf16), g[q + 1].astype(bf16)], axis=1)
            product = jnp.dot(stiff, both, preferred_element_type=f32)
            for h in range(2):
                cell = base + 2 * (q + h)
                one = jnp.where(cell < live, scale_ref[cell], 0.0)
                two = jnp.where(cell + 1 < live, scale_ref[cell + 1], 0.0)
                p[q + h] = product[:, h * LANES : (h + 1) * LANES] * jnp.where(left, one, two)

        def step(i):
            scatter(i, base)
            gather(i, following)

        each_row(step)
        return carry

    lax.fori_loop(0, (live + GROUP - 1) // GROUP, one_group, 0)

    def total(first, count):
        one = acc[0][pl.ds(first, count), :]
        two = acc[1][pl.ds(first, count), :]
        for q in range(1, PAIRS):
            one = one + acc[2 * q][pl.ds(first, count), :]
            two = two + acc[2 * q + 1][pl.ds(first, count), :]
        both = jnp.where(left, one, two)
        return both + swap(both)

    return total


def cells_kernel(
    live_ref, index_ref, scale_ref, stiff_ref, own_ref, low_ref, high_ref,
    sums_ref, sums_low_ref, sums_high_ref, x, g, p, *acc
):
    total = cell_sums(live_ref, index_ref, scale_ref, stiff_ref, own_ref, low_ref, high_ref, x, g, p, acc)
    ghost = 2 * low_ref.shape[0]
    owned = own_ref.shape[0]
    sums_ref[...] = total(ghost, owned)
    sums_low_ref[...] = pack(total(0, ghost))
    sums_high_ref[...] = pack(total(ghost + owned, ghost))


def last_cells_kernel(
    live_ref, index_ref, scale_ref, stiff_ref, own_ref, low_ref, high_ref, local_ref,
    packed_ref, x, g, p, *acc
):
    total = cell_sums(live_ref, index_ref, scale_ref, stiff_ref, own_ref, low_ref, high_ref, x, g, p, acc)
    ghost = 2 * low_ref.shape[0]
    owned = own_ref.shape[0]
    half = ghost // 2
    packed_ref[pl.ds(0, half), :] = pack(total(0, ghost))
    for m in range(owned // ghost):
        part = total(ghost + m * ghost, ghost) + local_ref[pl.ds(m * ghost, ghost), :]
        packed_ref[pl.ds(half + m * half, half), :] = pack(part)
    packed_ref[pl.ds(half + owned // 2, half), :] = pack(total(ghost + owned, ghost))


def assembled(shared_ref, sums_ref, lower_ref, upper_ref, acc):
    left = left_lanes()
    count = lower_ref.shape[0]
    for a in acc:
        a[...] = jnp.zeros_like(a)

    def some(turn, carry):
        for step in range(8):
            k = turn * 8 + step
            for side, ref in ((0, lower_ref), (1, upper_ref)):
                row = ref[pl.ds(k, 1), :]
                for part in range(2):
                    at = shared_ref[2 * count * side + count * part + k]
                    acc[2 * side + part][pl.ds(at, 1), :] += row
        return carry

    lax.fori_loop(0, count // 8, some, 0)
    both = jnp.where(left, acc[0][...] + acc[2][...], acc[1][...] + acc[3][...])
    return sums_ref[...] + (both + swap(both))


def first_kernel(
    shared_ref, window_ref, sums_ref, lower_ref, upper_ref, waves_ref, potential_ref,
    rows_ref, low_ref, high_ref, stage, *acc
):
    waves = waves_ref[...]
    applied = assembled(shared_ref, sums_ref, lower_ref, upper_ref, acc) + potential_ref[...] * waves
    first = (applied - window_ref[0] * waves) * window_ref[1]
    rows_ref[...] = first.astype(bf16).astype(f32)
    send_lists(rows_ref, shared_ref, low_ref, high_ref, stage)


def second_kernel(
    shared_ref, window_ref, sums_ref, lower_ref, upper_ref, waves_ref, first_ref, potential_ref,
    rows_ref, low_ref, high_ref, packed_ref, local_ref, filtered_ref, stage, *acc
):
    first = first_ref[...]
    potential = potential_ref[...]
    applied = assembled(shared_ref, sums_ref, lower_ref, upper_ref, acc) + potential * first
    filtered = (applied - window_ref[0] * first) * window_ref[2] - (sigma_one * sigma_two) * waves_ref[...]
    rounded = filtered.astype(bf16).astype(f32)
    rows_ref[...] = rounded
    send_lists(rows_ref, shared_ref, low_ref, high_ref, stage)
    local_ref[...] = potential * filtered
    half = low_ref.shape[0]
    for m in range(rounded.shape[0] // (2 * half)):
        part = pack(rounded[2 * half * m : 2 * half * (m + 1)])
        packed_ref[pl.ds(half * m, half), :] = part.astype(bf16)
    filtered_ref[...] = jnp.transpose(filtered)[:HALF]


def product_kernel(band_ref, sums_ref, *refs):
    parts, (out_ref, product) = refs[:-2], refs[-2:]
    turned = jnp.transpose(sums_ref[...])
    coarse = turned.astype(bf16)
    fine = (turned - coarse.astype(f32)).astype(bf16)
    left_side = jnp.concatenate([coarse, fine], axis=0)
    bands = len(parts) // 3
    for shift in range(bands):
        at = lax.rem(band_ref[0] + shift, bands) * HALF
        block = jnp.concatenate([ref[...] for ref in parts[3 * shift : 3 * shift + 3]], axis=0)
        both = jnp.dot(left_side, block, preferred_element_type=f32)
        both = both[:LANES] + both[LANES:]
        square = jnp.transpose(both + swap(pltpu.roll(both, HALF, 0)))
        product[pl.ds(pl.multiple_of(at, HALF), HALF), :] = square[:HALF]
    left = left_lanes()
    chunks = product.shape[0] // 4
    four = [product[pl.ds(r, chunks, stride=4), :] for r in range(4)]
    out_ref[:, 0:LANES] = jnp.where(left, four[0], swap(four[1]))
    out_ref[:, LANES : 2 * LANES] = jnp.where(left, four[2], swap(four[3]))


def local(waves, stiffness, cell_scale, potential, connect, live_cells, shared, window):
    columns, owned = waves.shape
    ghost = shared.shape[2]
    half = ghost // 2
    extended = owned + 2 * ghost
    nodes = connect.shape[0]
    cell_count = lax.axis_size("cells")
    band_count = lax.axis_size("bands")
    shared_list = shared.reshape(-1)
    index = connect.reshape(-1)
    stiff = jnp.pad(stiffness.astype(bf16), ((0, LANES - nodes), (0, LANES - nodes)))
    numbers = jnp.stack([window[0], sigma_one / window[1], 2.0 * sigma_two / window[1]])
    potential_rows = jnp.broadcast_to(potential[:, None], (owned, LANES))
    forward = [(i, i + 1) for i in range(cell_count - 1)]
    backward = [(target, source) for source, target in forward]

    def exchange(low, high):
        return lax.ppermute(high, "cells", forward), lax.ppermute(low, "cells", backward)

    rows_of = shape_of(owned, LANES, f32)
    list_of = shape_of(half, LANES, bf16)
    stage_of = pltpu.VMEM((half, LANES), f32)
    cell_scratch = [
        pltpu.VMEM((extended, LANES), f32),
        pltpu.VMEM((PAIRS, LANES, LANES), f32),
        pltpu.VMEM((PAIRS, LANES, LANES), f32),
    ] + [pltpu.VMEM((extended, LANES), f32)] * GROUP
    node_scratch = [stage_of] + [pltpu.VMEM((owned, LANES), f32)] * 4

    def call(kernel, outs, scratch, smem, vmem, name):
        return pl.pallas_call(
            kernel,
            out_shape=outs,
            in_specs=[SMEM] * len(smem) + [VMEM] * len(vmem),
            out_specs=jax.tree.map(lambda _: VMEM, outs),
            scratch_shapes=scratch,
            compiler_params=PARAMS,
            name=name,
        )(*smem, *vmem)

    waves_rows, low, high = call(
        prepare_kernel, (rows_of, list_of, list_of), [stage_of], (shared_list,), (waves,), "prepare"
    )
    tables = (live_cells, index, cell_scale)
    edge_of = shape_of(half, LANES, f32)

    def cells(rows, below, above):
        sums, sums_low, sums_high = call(
            cells_kernel, (rows_of, edge_of, edge_of), cell_scratch, tables, (stiff, rows, below, above), "cells"
        )
        lower, upper = exchange(sums_low, sums_high)
        return sums, lower, upper

    below, above = exchange(low, high)
    sums, lower, upper = cells(waves_rows, below, above)
    first_rows, low, high = call(
        first_kernel, (rows_of, list_of, list_of), node_scratch, (shared_list, numbers),
        (sums, lower, upper, waves_rows, potential_rows), "first",
    )
    below, above = exchange(low, high)
    sums, lower, upper = cells(first_rows, below, above)
    rounded_rows, low, high, packed, local_rows, filtered = call(
        second_kernel,
        (rows_of, list_of, list_of, shape_of(owned // 2, LANES, bf16), rows_of, shape_of(columns, owned, f32)),
        node_scratch, (shared_list, numbers),
        (sums, lower, upper, waves_rows, first_rows, potential_rows), "second",
    )
    below, above = exchange(low, high)
    parts = [below, packed, above]
    for shift in range(1, band_count):
        turn = [((b + shift) % band_count, b) for b in range(band_count)]
        parts += [lax.ppermute(part, "bands", turn) for part in (below, packed, above)]
    packed_sums = call(
        last_cells_kernel, shape_of(extended // 2, LANES, f32), cell_scratch, tables,
        (stiff, rounded_rows, below, above, local_rows), "last_cells",
    )
    band = lax.axis_index("bands").reshape(1).astype(jnp.int32)
    waves_all = columns * band_count
    partial_value = call(
        product_kernel, shape_of(waves_all // 4, 4 * HALF, f32),
        [pltpu.VMEM((waves_all, LANES), f32)], (band,), (packed_sums, *parts), "product",
    )
    arrived = lax.all_to_all(partial_value, "cells", split_axis=0, concat_axis=0, tiled=True)
    own_rows = waves_all // cell_count
    projected = (arrived.sum(axis=0) * (1.0 / (owned * cell_count))).reshape(own_rows, columns)
    return (filtered, projected)


def solution(mesh):
    return jax.shard_map(
        local,
        mesh=mesh,
        in_specs=(
            P("bands", "cells"),
            P(),
            P("cells"),
            P("cells"),
            P(None, "cells"),
            P("cells"),
            P("cells", None, None),
            P(),
        ),
        out_specs=(P("bands", "cells"), P("cells", "bands")),
        check_vma=False,
    )
```

time: 886 us -> 240 us (0.27)
  other arithmetic: 301 us -> 1.42 us
  waiting for transfers between devices: 289 us -> 28.7 us
  local copies, waits for them, and re-layouts: 195 us -> 8.13 us
  Pallas kernels: 0 us -> 57.8 us
  blocking collectives: 19.3 us -> 70.8 us
  starting transfers between devices: 45.7 us -> 66.4 us
  between operations: 16.8 us -> 2.69 us
  matrix products: 9.85 us -> 0 us
    scatter-add x9 -> x0, other arithmetic: 292 us -> none  [the longest x3 266 us: one_block(): totals.at[:, connect.reshape(-1)]]
    unnamed x2 -> x0, waiting for transfers between devices: 275 us -> none
    gather x12 -> x0, local copies, waits for them, and re-layouts: 130 us -> none  [the longest x6 121 us: one_block(): gathered = extended[:, connect]]
    pallas_call x0 -> x7, Pallas kernels: none -> 57.8 us  [call(): pl.pallas_call(kernel, out_shape=outs, in_specs=[SMEM] * len(smem) + [VME...]
    all_to_all x1, blocking collectives: 19.3 us -> 70.8 us  [local(): lax.all_to_all(partial_value, 'cells', split_axis=0, concat_axis=0, tiled...]
    ppermute x12 -> x19, starting transfers between devices: 38.1 us -> 66.4 us  [the longest x9 27.1 us: local(): lax.ppermute(part, 'bands', turn)]
    reshape x4 -> x0, local copies, waits for them, and re-layouts: 20.6 us -> none  [the longest x3 20.4 us: one_block(): (product * weight[None, None, :]).reshape(columns, -1)]
    unnamed x28 -> x45, local copies, waits for them, and re-layouts: 23.6 us -> 4.07 us
  transfers between devices with their start and end apart: 14 -> 19, of which waited for: 10 -> 9; matrix products, arithmetic and copies ran while one was open for 21% -> 1% of each run, Pallas kernels for 0% -> 5%
where the time goes in v1:
time: 240 us; the launch traced here: 236 us
  blocking collectives  70.8 us (30%)
  starting transfers between devices  66.4 us (28%)
  Pallas kernels  57.8 us (24%)
  waiting for transfers between devices  28.7 us (12%)
  local copies, waits for them, and re-layouts  8.13 us (3%)
  between operations  2.69 us (1%)
    all_to_all x1, blocking collectives, local(): lax.all_to_all(partial_value, 'cells', split_axis=0, concat_axis=0, tiled...  70.8 us
    pallas_call x7, Pallas kernels, call(): pl.pallas_call(kernel, out_shape=outs, in_specs=[SMEM] * len(smem) + [VME...  57.8 us
    ppermute x9, starting transfers between devices, local(): lax.ppermute(part, 'bands', turn)  27.1 us
    ppermute x5, starting transfers between devices, exchange(): lax.ppermute(high, 'cells', forward)  26.5 us
    ppermute x9, waiting for transfers between devices, local(): lax.ppermute(part, 'bands', turn)  13.8 us
    ppermute x5, waiting for transfers between devices, exchange(): lax.ppermute(low, 'cells', backward)  13.5 us
    ppermute x5, starting transfers between devices, exchange(): lax.ppermute(low, 'cells', backward)  12.8 us
  transfers between devices with their start and end apart: 19, of which 9 were waited for; matrix products, arithmetic and copies ran while one was open for 1% of the time, Pallas kernels for 5%

profile of v1, /device:TPU:2, one launch (start us, length us, event | category | flops | bytes accessed | tf_op | source)
XLA Modules:
  0.0 235.9 jit_solution(8940743245998472491)
XLA Ops:
  0.6 1.3 copy.11
  1.9 3.3 %prepare.1 = (f32[2048,128]{1,0:T(8,128)}, bf16[256,128]{1,0:T(8,128)(2,1)}, bf16[256,128]{1,0:T(8,128)(2,1)}) custom-call(s32[1024]{0:T(1024)} %bitcast.9, bf16[64,2048]{1,0:T(8,128)(2,1)} %waves_ref.1), custom_call_target="tpu_custom_call" | custom-call | tf_op jit(solution)/shard_map/prepare/pallas_call | solution.py:277
  5.2 3.4 %collective-permute-start = (bf16[256,128]{1,0:T(8,128)(2,1)}, bf16[256,128]{1,0:T(8,128)(2,1)S(1)}, u32[]{:S(2)}, u32[]{:S(2)}) collective-permute-start(bf16[256,128]{1,0:T(8,128)(2,1)} %get-tuple-element.21), channel_id=1, source_target_pairs={{0,4},{4,8},{8,12},{12,16},{16,20},{20,24},{24,28},{28,32},{32,36}... | collective-permute-start | bytes 196616 | tf_op jit(solution)/shard_map/ppermute | solution.py:264
  8.6 2.4 %collective-permute-start.1 = (bf16[256,128]{1,0:T(8,128)(2,1)}, bf16[256,128]{1,0:T(8,128)(2,1)S(1)}, u32[]{:S(2)}, u32[]{:S(2)}) collective-permute-start(bf16[256,128]{1,0:T(8,128)(2,1)} %get-tuple-element.22), channel_id=1, source_target_pairs={{4,0},{8,4},{12,8},{16,12},{20,16},{24,20},{28,24},{32,28},{36,32}... | collective-permute-start | bytes 196616 | tf_op jit(solution)/shard_map/ppermute | solution.py:264
  12.4 2.6 %collective-permute-done.1.high_ref = bf16[256,128]{1,0:T(8,128)(2,1)S(1)} collective-permute-done((bf16[256,128]{1,0:T(8,128)(2,1)}, bf16[256,128]{1,0:T(8,128)(2,1)S(1)}, u32[]{:S(2)}, u32[]{:S(2)}) %collective-permute-start.1) | collective-permute-done | bytes 65568 | tf_op jit(solution)/shard_map/ppermute | solution.py:264
  15.6 12.4 %cells.2 = (f32[2048,128]{1,0:T(8,128)}, f32[256,128]{1,0:T(8,128)}, f32[256,128]{1,0:T(8,128)}) custom-call(s32[1]{0:T(128)S(6)} %copy.12.live_ref, s32[16000]{0:T(1024)} %bitcast.5, f32[128]{0:T(128)} %scale_ref.5, bf16[128,128]{1,0:T(8,128)(2,1)} %pad.4.stiff_ref, f32[2048,128]{1,0:T(8,128)} %get-tuple-element.20.own_ref.waves_ref, ...), custom_call_target="tpu_custom_call" | custom-call | tf_op jit(solution)/shard_map/cells/pallas_call | solution.py:277
  28.0 8.7 %collective-permute-start.2 = (f32[256,128]{1,0:T(8,128)}, f32[256,128]{1,0:T(8,128)S(1)}, u32[]{:S(2)}, u32[]{:S(2)}) collective-permute-start(f32[256,128]{1,0:T(8,128)} %get-tuple-element.24), channel_id=1, source_target_pairs={{0,4},{4,8},{8,12},{12,16},{16,20},{20,24},{24,28},{28,32},{32,36}... | collective-permute-start | bytes 393224 | tf_op jit(solution)/shard_map/ppermute | solution.py:264
  36.7 1.9 collective-permute-start.3
  40.3 1.3 pad_maximum_fusion.window_ref
  41.6 2.1 collective-permute-done.3.upper_ref
  43.7 1.3 broadcast_in_dim.2.potential_ref
  45.1 6.3 %first.1 = (f32[2048,128]{1,0:T(8,128)}, bf16[256,128]{1,0:T(8,128)(2,1)}, bf16[256,128]{1,0:T(8,128)(2,1)}) custom-call(s32[1024]{0:T(1024)} %bitcast.10, f32[3]{0:T(128)} %pad_maximum_fusion.window_ref, f32[2048,128]{1,0:T(8,128)} %get-tuple-element.23.sums_ref, f32[256,128]{1,0:T(8,128)} %copy-done.5, f32[256,128]{1,0:T(8,128)} %copy-done.6, ...), custom_call_target="tpu_custom_call" | custom-call | tf_op jit(solution)/shard_map/first/pallas_call | solution.py:277
  51.4 1.9 collective-permute-start.4
  53.3 3.9 %collective-permute-start.5 = (bf16[256,128]{1,0:T(8,128)(2,1)}, bf16[256,128]{1,0:T(8,128)(2,1)S(1)}, u32[]{:S(2)}, u32[]{:S(2)}) collective-permute-start(bf16[256,128]{1,0:T(8,128)(2,1)} %get-tuple-element.28), channel_id=1, source_target_pairs={{4,0},{8,4},{12,8},{16,12},{20,16},{24,20},{28,24},{32,28},{36,32}... | collective-permute-start | bytes 196616 | tf_op jit(solution)/shard_map/ppermute | solution.py:264
  57.8 4.5 %collective-permute-done.5.high_ref = bf16[256,128]{1,0:T(8,128)(2,1)S(1)} collective-permute-done((bf16[256,128]{1,0:T(8,128)(2,1)}, bf16[256,128]{1,0:T(8,128)(2,1)S(1)}, u32[]{:S(2)}, u32[]{:S(2)}) %collective-permute-start.5) | collective-permute-done | bytes 65568 | tf_op jit(solution)/shard_map/ppermute | solution.py:264
  62.9 12.4 %cells.3 = (f32[2048,128]{1,0:T(8,128)}, f32[256,128]{1,0:T(8,128)}, f32[256,128]{1,0:T(8,128)}) custom-call(s32[1]{0:T(128)S(6)} %copy.12.live_ref, s32[16000]{0:T(1024)} %bitcast.6, f32[128]{0:T(128)} %scale_ref.5, bf16[128,128]{1,0:T(8,128)(2,1)} %pad.4.stiff_ref, f32[2048,128]{1,0:T(8,128)} %get-tuple-element.26.own_ref.first_ref, ...), custom_call_target="tpu_custom_call" | custom-call | tf_op jit(solution)/shard_map/cells/pallas_call | solution.py:277
  75.2 9.3 %collective-permute-start.6 = (f32[256,128]{1,0:T(8,128)}, f32[256,128]{1,0:T(8,128)S(1)}, u32[]{:S(2)}, u32[]{:S(2)}) collective-permute-start(f32[256,128]{1,0:T(8,128)} %get-tuple-element.30), channel_id=1, source_target_pairs={{0,4},{4,8},{8,12},{12,16},{16,20},{20,24},{24,28},{28,32},{32,36}... | collective-permute-start | bytes 393224 | tf_op jit(solution)/shard_map/ppermute | solution.py:264
  84.6 1.9 collective-permute-start.7
  87.4 4.3 %collective-permute-done.7.upper_ref = f32[256,128]{1,0:T(8,128)S(1)} collective-permute-done((f32[256,128]{1,0:T(8,128)}, f32[256,128]{1,0:T(8,128)S(1)}, u32[]{:S(2)}, u32[]{:S(2)}) %collective-permute-start.7) | collective-permute-done | bytes 131104 | tf_op jit(solution)/shard_map/ppermute | solution.py:264
  92.3 7.4 %second.1 = (f32[2048,128]{1,0:T(8,128)}, bf16[256,128]{1,0:T(8,128)(2,1)}, bf16[256,128]{1,0:T(8,128)(2,1)}, bf16[1024,128]{1,0:T(8,128)(2,1)}, f32[2048,128]{1,0:T(8,128)}, /*index=5*/f32[64,2048]{1,0:T(8,128)}) custom-call(s32[1024]{0:T(1024)} %bitcast.11, f32[3]{0:T(128)} %pad_maximum_fusion.window_ref, f32[2048,128]{1,0:T(8,128)} %get-tuple-element.29.sums_ref, ...), custom_call_target="tpu_custom_call" | custom-call | tf_op jit(solution)/shard_map/second/pallas_call | solution.py:277
  99.7 3.2 %collective-permute-start.8 = (bf16[256,128]{1,0:T(8,128)(2,1)}, bf16[256,128]{1,0:T(8,128)(2,1)S(1)}, u32[]{:S(2)}, u32[]{:S(2)}) collective-permute-start(bf16[256,128]{1,0:T(8,128)(2,1)} %get-tuple-element.34), channel_id=1, source_target_pairs={{0,4},{4,8},{8,12},{12,16},{16,20},{20,24},{24,28},{28,32},{32,36}... | collective-permute-start | bytes 196616 | tf_op jit(solution)/shard_map/ppermute | solution.py:264
  102.9 2.6 %collective-permute-start.9 = (bf16[256,128]{1,0:T(8,128)(2,1)}, bf16[256,128]{1,0:T(8,128)(2,1)S(1)}, u32[]{:S(2)}, u32[]{:S(2)}) collective-permute-start(bf16[256,128]{1,0:T(8,128)(2,1)} %get-tuple-element.35), channel_id=1, source_target_pairs={{4,0},{8,4},{12,8},{16,12},{20,16},{24,20},{28,24},{32,28},{36,32}... | collective-permute-start | bytes 196616 | tf_op jit(solution)/shard_map/ppermute | solution.py:264
  105.7 6.4 %collective-permute-start.14 = (bf16[1024,128]{1,0:T(8,128)(2,1)}, bf16[1024,128]{1,0:T(8,128)(2,1)S(1)}, u32[]{:S(2)}, u32[]{:S(2)}) collective-permute-start(bf16[1024,128]{1,0:T(8,128)(2,1)} %get-tuple-element.37.refs_1_), channel_id=1, source_target_pairs={{2,0},{3,1},{0,2},{1,3},{6,4},{7,5},{4,6},{5,7},{10,8},{11,9},{8,1... | collective-permute-start | bytes 786440 | tf_op jit(solution)/shard_map/ppermute | solution.py:318
  112.2 5.5 %collective-permute-start.10 = (bf16[256,128]{1,0:T(8,128)(2,1)S(1)}, bf16[256,128]{1,0:T(8,128)(2,1)S(1)}, u32[]{:S(2)}, u32[]{:S(2)}) collective-permute-start(bf16[256,128]{1,0:T(8,128)(2,1)S(1)} %collective-permute-done.8.low_ref.refs_0_), channel_id=1, source_target_pairs={{1,0},{2,1},{3,2},{0,3},{5,4},{6,5},{7,6},{4,7},{9,8},{10,9},{11,1... | collective-permute-start | bytes 196616 | tf_op jit(solution)/shard_map/ppermute | solution.py:318
  117.8 4.0 %collective-permute-done.10.refs_3_ = bf16[256,128]{1,0:T(8,128)(2,1)S(1)} collective-permute-done((bf16[256,128]{1,0:T(8,128)(2,1)S(1)}, bf16[256,128]{1,0:T(8,128)(2,1)S(1)}, u32[]{:S(2)}, u32[]{:S(2)}) %collective-permute-start.10) | collective-permute-done | bytes 65568 | tf_op jit(solution)/shard_map/ppermute | solution.py:318
  121.8 7.9 %collective-permute-start.13 = (bf16[256,128]{1,0:T(8,128)(2,1)S(1)}, bf16[256,128]{1,0:T(8,128)(2,1)S(1)}, u32[]{:S(2)}, u32[]{:S(2)}) collective-permute-start(bf16[256,128]{1,0:T(8,128)(2,1)S(1)} %collective-permute-done.8.low_ref.refs_0_), channel_id=1, source_target_pairs={{2,0},{3,1},{0,2},{1,3},{6,4},{7,5},{4,6},{5,7},{10,8},{11,9},{8,1... | collective-permute-start | bytes 196616 | tf_op jit(solution)/shard_map/ppermute | solution.py:318
  130.4 9.6 %collective-permute-done.13.refs_6_ = bf16[256,128]{1,0:T(8,128)(2,1)S(1)} collective-permute-done((bf16[256,128]{1,0:T(8,128)(2,1)S(1)}, bf16[256,128]{1,0:T(8,128)(2,1)S(1)}, u32[]{:S(2)}, u32[]{:S(2)}) %collective-permute-start.13) | collective-permute-done | bytes 65568 | tf_op jit(solution)/shard_map/ppermute | solution.py:318
  140.0 1.3 collective-permute-start.16
  141.5 4.9 %collective-permute-start.18 = (bf16[256,128]{1,0:T(8,128)(2,1)S(1)}, bf16[256,128]{1,0:T(8,128)(2,1)S(1)}, u32[]{:S(2)}, u32[]{:S(2)}) collective-permute-start(bf16[256,128]{1,0:T(8,128)(2,1)S(1)} %collective-permute-done.9.high_ref.refs_2_), channel_id=1, source_target_pairs={{3,0},{0,1},{1,2},{2,3},{7,4},{4,5},{5,6},{6,7},{11,8},{8,9},{9,10... | collective-permute-start | bytes 196616 | tf_op jit(solution)/shard_map/ppermute | solution.py:318
  146.4 12.5 %last_cells.1.sums_ref = f32[1536,128]{1,0:T(8,128)} custom-call(s32[1]{0:T(128)S(6)} %copy.12.live_ref, s32[16000]{0:T(1024)} %bitcast.7, f32[128]{0:T(128)} %scale_ref.5, bf16[128,128]{1,0:T(8,128)(2,1)} %pad.4.stiff_ref, f32[2048,128]{1,0:T(8,128)} %get-tuple-element.33.own_ref, bf16[256,128]{1,0:T(8,128)(2,1)} %copy-done.3, bf16[256,128]{1,0:T(8,128)(2,1)} %copy-done.4, ...), custom_call_target="tpu_custom_call" | custom-call | tf_op jit(solution)/shard_map/last_cells/pallas_call | solution.py:277
  159.9 3.5 %product.1 = f32[64,256]{1,0:T(8,128)} custom-call(s32[1]{0:T(128)} %bitcast.1.band_ref, f32[1536,128]{1,0:T(8,128)} %last_cells.1.sums_ref, bf16[256,128]{1,0:T(8,128)(2,1)} %copy-done.3, bf16[1024,128]{1,0:T(8,128)(2,1)} %get-tuple-element.37.refs_1_, bf16[256,128]{1,0:T(8,128)(2,1)} %copy-done.4, bf16[256,128]{1,0:T(8,128)(2,1)} %copy-done.14, ...), custom_call_target="tpu_custom_call" | custom-call | tf_op jit(solution)/shard_map/product/pallas_call | solution.py:277
  164.3 70.8 %all_to_all.9 = f32[64,1,256]{2,1,0:T(1,128)S(1)} all-to-all(f32[64,1,256]{2,1,0:T(1,128)S(1)} %copy.10), channel_id=1, replica_groups=mesh['cells'=64,'bands'=4] {'cells'}, dimensions={0} | all-to-all | bytes 131072 | tf_op jit(solution)/shard_map/all_to_all | solution.py:329
  (68 shorter events, 8.2 us)
Async XLA Ops:
  1.9 9.2 %copy-start.13 = (f32[125,125]{1,0:T(8,128)S(1)}, f32[125,125]{1,0:T(8,128)}, u32[]{:S(2)}) copy-start(f32[125,125]{1,0:T(8,128)} %param.9) | copy-start | bytes 187504
  5.2 7.1 %collective-permute-start = (bf16[256,128]{1,0:T(8,128)(2,1)}, bf16[256,128]{1,0:T(8,128)(2,1)S(1)}, u32[]{:S(2)}, u32[]{:S(2)}) collective-permute-start(bf16[256,128]{1,0:T(8,128)(2,1)} %get-tuple-element.21), channel_id=1, source_target_pairs={{0,4},{4,8},{8,12},{12,16},{16,20},{20,24},{24,28},{28,32},{32,36}... | collective-permute-start | bytes 196616 | tf_op jit(solution)/shard_map/ppermute | solution.py:264
  8.6 6.4 %collective-permute-start.1 = (bf16[256,128]{1,0:T(8,128)(2,1)}, bf16[256,128]{1,0:T(8,128)(2,1)S(1)}, u32[]{:S(2)}, u32[]{:S(2)}) collective-permute-start(bf16[256,128]{1,0:T(8,128)(2,1)} %get-tuple-element.22), channel_id=1, source_target_pairs={{4,0},{8,4},{12,8},{16,12},{20,16},{24,20},{28,24},{32,28},{36,32}... | collective-permute-start | bytes 196616 | tf_op jit(solution)/shard_map/ppermute | solution.py:264
  12.4 2.6 %copy-start.9 = (bf16[256,128]{1,0:T(8,128)(2,1)}, bf16[256,128]{1,0:T(8,128)(2,1)S(1)}, u32[]{:S(2)}) copy-start(bf16[256,128]{1,0:T(8,128)(2,1)S(1)} %collective-permute-done.low_ref) | copy-start | bytes 196612
  28.0 10.6 %copy-start.21 = (f32[2]{0:T(128)S(1)}, f32[2]{0:T(128)}, u32[]{:S(2)}) copy-start(f32[2]{0:T(128)} %param.15) | copy-start | bytes 28
  28.0 15.8 %copy-start.20 = (f32[2048]{0:T(1024)S(1)}, f32[2048]{0:T(1024)}, u32[]{:S(2)}) copy-start(f32[2048]{0:T(1024)} %param.11) | copy-start | bytes 24580
  28.0 13.7 %collective-permute-start.2 = (f32[256,128]{1,0:T(8,128)}, f32[256,128]{1,0:T(8,128)S(1)}, u32[]{:S(2)}, u32[]{:S(2)}) collective-permute-start(f32[256,128]{1,0:T(8,128)} %get-tuple-element.24), channel_id=1, source_target_pairs={{0,4},{4,8},{8,12},{12,16},{16,20},{20,24},{24,28},{28,32},{32,36}... | collective-permute-start | bytes 393224 | tf_op jit(solution)/shard_map/ppermute | solution.py:264
  36.7 7.1 %collective-permute-start.3 = (f32[256,128]{1,0:T(8,128)}, f32[256,128]{1,0:T(8,128)S(1)}, u32[]{:S(2)}, u32[]{:S(2)}) collective-permute-start(f32[256,128]{1,0:T(8,128)} %get-tuple-element.25), channel_id=1, source_target_pairs={{4,0},{8,4},{12,8},{16,12},{20,16},{24,20},{28,24},{32,28},{36,32}... | collective-permute-start | bytes 393224 | tf_op jit(solution)/shard_map/ppermute | solution.py:264
  41.6 3.4 %copy-start.5 = (f32[256,128]{1,0:T(8,128)}, f32[256,128]{1,0:T(8,128)S(1)}, u32[]{:S(2)}) copy-start(f32[256,128]{1,0:T(8,128)S(1)} %collective-permute-done.2.lower_ref) | copy-start | bytes 393220
  51.4 6.4 %collective-permute-start.4 = (bf16[256,128]{1,0:T(8,128)(2,1)}, bf16[256,128]{1,0:T(8,128)(2,1)S(1)}, u32[]{:S(2)}, u32[]{:S(2)}) collective-permute-start(bf16[256,128]{1,0:T(8,128)(2,1)} %get-tuple-element.27), channel_id=1, source_target_pairs={{0,4},{4,8},{8,12},{12,16},{16,20},{20,24},{24,28},{28,32},{32,36}... | collective-permute-start | bytes 196616 | tf_op jit(solution)/shard_map/ppermute | solution.py:264
  53.3 9.0 %collective-permute-start.5 = (bf16[256,128]{1,0:T(8,128)(2,1)}, bf16[256,128]{1,0:T(8,128)(2,1)S(1)}, u32[]{:S(2)}, u32[]{:S(2)}) collective-permute-start(bf16[256,128]{1,0:T(8,128)(2,1)} %get-tuple-element.28), channel_id=1, source_target_pairs={{4,0},{8,4},{12,8},{16,12},{20,16},{24,20},{28,24},{32,28},{36,32}... | collective-permute-start | bytes 196616 | tf_op jit(solution)/shard_map/ppermute | solution.py:264
  57.7 4.5 %copy-start.11 = (bf16[256,128]{1,0:T(8,128)(2,1)}, bf16[256,128]{1,0:T(8,128)(2,1)S(1)}, u32[]{:S(2)}) copy-start(bf16[256,128]{1,0:T(8,128)(2,1)S(1)} %collective-permute-done.4.low_ref) | copy-start | bytes 196612
  75.2 12.2 %collective-permute-start.6 = (f32[256,128]{1,0:T(8,128)}, f32[256,128]{1,0:T(8,128)S(1)}, u32[]{:S(2)}, u32[]{:S(2)}) collective-permute-start(f32[256,128]{1,0:T(8,128)} %get-tuple-element.30), channel_id=1, source_target_pairs={{0,4},{4,8},{8,12},{12,16},{16,20},{20,24},{24,28},{28,32},{32,36}... | collective-permute-start | bytes 393224 | tf_op jit(solution)/shard_map/ppermute | solution.py:264
  84.6 7.1 %collective-permute-start.7 = (f32[256,128]{1,0:T(8,128)}, f32[256,128]{1,0:T(8,128)S(1)}, u32[]{:S(2)}, u32[]{:S(2)}) collective-permute-start(f32[256,128]{1,0:T(8,128)} %get-tuple-element.31), channel_id=1, source_target_pairs={{4,0},{8,4},{12,8},{16,12},{20,16},{24,20},{28,24},{32,28},{36,32}... | collective-permute-start | bytes 393224 | tf_op jit(solution)/shard_map/ppermute | solution.py:264
  87.4 4.3 %copy-start.7 = (f32[256,128]{1,0:T(8,128)}, f32[256,128]{1,0:T(8,128)S(1)}, u32[]{:S(2)}) copy-start(f32[256,128]{1,0:T(8,128)S(1)} %collective-permute-done.6.lower_ref) | copy-start | bytes 393220
  99.7 12.4 %collective-permute-start.8 = (bf16[256,128]{1,0:T(8,128)(2,1)}, bf16[256,128]{1,0:T(8,128)(2,1)S(1)}, u32[]{:S(2)}, u32[]{:S(2)}) collective-permute-start(bf16[256,128]{1,0:T(8,128)(2,1)} %get-tuple-element.34), channel_id=1, source_target_pairs={{0,4},{4,8},{8,12},{12,16},{16,20},{20,24},{24,28},{28,32},{32,36}... | collective-permute-start | bytes 196616 | tf_op jit(solution)/shard_map/ppermute | solution.py:264
  102.9 14.8 %collective-permute-start.9 = (bf16[256,128]{1,0:T(8,128)(2,1)}, bf16[256,128]{1,0:T(8,128)(2,1)S(1)}, u32[]{:S(2)}, u32[]{:S(2)}) collective-permute-start(bf16[256,128]{1,0:T(8,128)(2,1)} %get-tuple-element.35), channel_id=1, source_target_pairs={{4,0},{8,4},{12,8},{16,12},{20,16},{24,20},{28,24},{32,28},{36,32}... | collective-permute-start | bytes 196616 | tf_op jit(solution)/shard_map/ppermute | solution.py:264
  105.6 53.5 %collective-permute-start.11 = (bf16[1024,128]{1,0:T(8,128)(2,1)}, bf16[1024,128]{1,0:T(8,128)(2,1)S(1)}, u32[]{:S(2)}, u32[]{:S(2)}) collective-permute-start(bf16[1024,128]{1,0:T(8,128)(2,1)} %get-tuple-element.37.refs_1_), channel_id=1, source_target_pairs={{1,0},{2,1},{3,2},{0,3},{5,4},{6,5},{7,6},{4,7},{9,8},{10,9},{11,1... | collective-permute-start | bytes 786440 | tf_op jit(solution)/shard_map/ppermute | solution.py:318
  105.7 53.4 %collective-permute-start.14 = (bf16[1024,128]{1,0:T(8,128)(2,1)}, bf16[1024,128]{1,0:T(8,128)(2,1)S(1)}, u32[]{:S(2)}, u32[]{:S(2)}) collective-permute-start(bf16[1024,128]{1,0:T(8,128)(2,1)} %get-tuple-element.37.refs_1_), channel_id=1, source_target_pairs={{2,0},{3,1},{0,2},{1,3},{6,4},{7,5},{4,6},{5,7},{10,8},{11,9},{8,1... | collective-permute-start | bytes 786440 | tf_op jit(solution)/shard_map/ppermute | solution.py:318
  112.0 47.0 %collective-permute-start.17 = (bf16[1024,128]{1,0:T(8,128)(2,1)}, bf16[1024,128]{1,0:T(8,128)(2,1)S(1)}, u32[]{:S(2)}, u32[]{:S(2)}) collective-permute-start(bf16[1024,128]{1,0:T(8,128)(2,1)} %get-tuple-element.37.refs_1_), channel_id=1, source_target_pairs={{3,0},{0,1},{1,2},{2,3},{7,4},{4,5},{5,6},{6,7},{11,8},{8,9},{9,10... | collective-permute-start | bytes 786440 | tf_op jit(solution)/shard_map/ppermute | solution.py:318
  112.2 34.3 %copy-start.3 = (bf16[256,128]{1,0:T(8,128)(2,1)}, bf16[256,128]{1,0:T(8,128)(2,1)S(1)}, u32[]{:S(2)}) copy-start(bf16[256,128]{1,0:T(8,128)(2,1)S(1)} %collective-permute-done.8.low_ref.refs_0_) | copy-start | bytes 196612
  112.2 9.7 %collective-permute-start.10 = (bf16[256,128]{1,0:T(8,128)(2,1)S(1)}, bf16[256,128]{1,0:T(8,128)(2,1)S(1)}, u32[]{:S(2)}, u32[]{:S(2)}) collective-permute-start(bf16[256,128]{1,0:T(8,128)(2,1)S(1)} %collective-permute-done.8.low_ref.refs_0_), channel_id=1, source_target_pairs={{1,0},{2,1},{3,2},{0,3},{5,4},{6,5},{7,6},{4,7},{9,8},{10,9},{11,1... | collective-permute-start | bytes 196616 | tf_op jit(solution)/shard_map/ppermute | solution.py:318
  117.7 28.8 %copy-start.4 = (bf16[256,128]{1,0:T(8,128)(2,1)}, bf16[256,128]{1,0:T(8,128)(2,1)S(1)}, u32[]{:S(2)}) copy-start(bf16[256,128]{1,0:T(8,128)(2,1)S(1)} %collective-permute-done.9.high_ref.refs_2_) | copy-start | bytes 196612
  117.7 12.0 %collective-permute-start.12 = (bf16[256,128]{1,0:T(8,128)(2,1)S(1)}, bf16[256,128]{1,0:T(8,128)(2,1)S(1)}, u32[]{:S(2)}, u32[]{:S(2)}) collective-permute-start(bf16[256,128]{1,0:T(8,128)(2,1)S(1)} %collective-permute-done.9.high_ref.refs_2_), channel_id=1, source_target_pairs={{1,0},{2,1},{3,2},{0,3},{5,4},{6,5},{7,6},{4,7},{9,8},{10,9},{11,1... | collective-permute-start | bytes 196616 | tf_op jit(solution)/shard_map/ppermute | solution.py:318
  121.8 37.1 %copy-start.14 = (bf16[256,128]{1,0:T(8,128)(2,1)}, bf16[256,128]{1,0:T(8,128)(2,1)S(1)}, u32[]{:S(2)}) copy-start(bf16[256,128]{1,0:T(8,128)(2,1)S(1)} %collective-permute-done.10.refs_3_) | copy-start | bytes 196612
  121.8 18.2 %collective-permute-start.13 = (bf16[256,128]{1,0:T(8,128)(2,1)S(1)}, bf16[256,128]{1,0:T(8,128)(2,1)S(1)}, u32[]{:S(2)}, u32[]{:S(2)}) collective-permute-start(bf16[256,128]{1,0:T(8,128)(2,1)S(1)} %collective-permute-done.8.low_ref.refs_0_), channel_id=1, source_target_pairs={{2,0},{3,1},{0,2},{1,3},{6,4},{7,5},{4,6},{5,7},{10,8},{11,9},{8,1... | collective-permute-start | bytes 196616 | tf_op jit(solution)/shard_map/ppermute | solution.py:318
  129.7 29.3 %copy-start.15 = (bf16[256,128]{1,0:T(8,128)(2,1)}, bf16[256,128]{1,0:T(8,128)(2,1)S(1)}, u32[]{:S(2)}) copy-start(bf16[256,128]{1,0:T(8,128)(2,1)S(1)} %collective-permute-done.12.refs_5_) | copy-start | bytes 196612
  129.7 11.8 %collective-permute-start.15 = (bf16[256,128]{1,0:T(8,128)(2,1)S(1)}, bf16[256,128]{1,0:T(8,128)(2,1)S(1)}, u32[]{:S(2)}, u32[]{:S(2)}) collective-permute-start(bf16[256,128]{1,0:T(8,128)(2,1)S(1)} %collective-permute-done.9.high_ref.refs_2_), channel_id=1, source_target_pairs={{2,0},{3,1},{0,2},{1,3},{6,4},{7,5},{4,6},{5,7},{10,8},{11,9},{8,1... | collective-permute-start | bytes 196616 | tf_op jit(solution)/shard_map/ppermute | solution.py:318
  140.0 19.0 %copy-start.16 = (bf16[256,128]{1,0:T(8,128)(2,1)}, bf16[256,128]{1,0:T(8,128)(2,1)S(1)}, u32[]{:S(2)}) copy-start(bf16[256,128]{1,0:T(8,128)(2,1)S(1)} %collective-permute-done.13.refs_6_) | copy-start | bytes 196612
  140.0 19.0 %collective-permute-start.16 = (bf16[256,128]{1,0:T(8,128)(2,1)S(1)}, bf16[256,128]{1,0:T(8,128)(2,1)S(1)}, u32[]{:S(2)}, u32[]{:S(2)}) collective-permute-start(bf16[256,128]{1,0:T(8,128)(2,1)S(1)} %collective-permute-done.8.low_ref.refs_0_), channel_id=1, source_target_pairs={{3,0},{0,1},{1,2},{2,3},{7,4},{4,5},{5,6},{6,7},{11,8},{8,9},{9,10... | collective-permute-start | bytes 196616 | tf_op jit(solution)/shard_map/ppermute | solution.py:318
  141.5 17.5 %copy-start.17 = (bf16[256,128]{1,0:T(8,128)(2,1)}, bf16[256,128]{1,0:T(8,128)(2,1)S(1)}, u32[]{:S(2)}) copy-start(bf16[256,128]{1,0:T(8,128)(2,1)S(1)} %collective-permute-done.15.refs_8_) | copy-start | bytes 196612
  141.5 17.5 %collective-permute-start.18 = (bf16[256,128]{1,0:T(8,128)(2,1)S(1)}, bf16[256,128]{1,0:T(8,128)(2,1)S(1)}, u32[]{:S(2)}, u32[]{:S(2)}) collective-permute-start(bf16[256,128]{1,0:T(8,128)(2,1)S(1)} %collective-permute-done.9.high_ref.refs_2_), channel_id=1, source_target_pairs={{3,0},{0,1},{1,2},{2,3},{7,4},{4,5},{5,6},{6,7},{11,8},{8,9},{9,10... | collective-permute-start | bytes 196616 | tf_op jit(solution)/shard_map/ppermute | solution.py:318
  (9 other events, 6.9 us)
